TPU v7x, 32 devices: a whole 2x2x4 slice. The times are simulated.
32 devices in a mesh: dp: 16 (over z, y, x), tensor: 2 (over core).
Axes of the slice: x: 2, y: 2, z: 4, core: 2. Of those that a mesh axis runs over, the one named last changes fastest.
Arguments:
- inputs: bfloat16 [16, 1024, 768], P(None, 'dp', 'tensor'), may hold values from -6 to 6
- lengths: int32 [16], replicated, may hold values from 1 to 1024, 12288 in all
- order: int32 [16], replicated, may hold values from 0 to 15, each once
- w_query: bfloat16 [768, 768], P(None, 'tensor'), may hold values from -0.3125 to 0.3125
- b_query: bfloat16 [768], P('tensor'), may hold values from -3 to 3
- w_key: bfloat16 [768, 768], P(None, 'tensor'), may hold values from -0.3125 to 0.3125
- w_value: bfloat16 [768, 768], P(None, 'tensor'), may hold values from -0.21875 to 0.21875
- b_value: bfloat16 [768], P('tensor'), may hold values from -3 to 3
- w_out: bfloat16 [768, 768], P('tensor'), may hold values from -0.875 to 0.875
- b_out: bfloat16 [768], P('tensor'), may hold values from -3 to 3
- gain_one: bfloat16 [768], P('tensor'), may hold values from 0.5 to 1.5
- shift_one: bfloat16 [768], P('tensor'), may hold values from -3 to 3
- w_up: bfloat16 [768, 3072], P(None, 'tensor'), may hold values from -0.21875 to 0.21875
- b_up: bfloat16 [3072], P('tensor'), may hold values from -3 to 3
- w_down: bfloat16 [3072, 768], P('tensor'), may hold values from -0.109375 to 0.109375
- b_down: bfloat16 [768], P('tensor'), may hold values from -3 to 3
- gain_two: bfloat16 [768], P('tensor'), may hold values from 0.5 to 1.5
- shift_two: bfloat16 [768], P('tensor'), may hold values from -3 to 3
- cotangent: bfloat16 [16, 1024, 768], P('dp', 'tensor'), may hold values from -6 to 6
Outputs:
- output: bfloat16 [16, 1024, 768], P('dp', 'tensor')
- input_grad: bfloat16 [16, 1024, 768], P(None, 'dp', 'tensor')
- grad_w_query: float32 [768, 768], P(None, 'tensor')
- grad_b_query: float32 [768], P('tensor')
- grad_w_key: float32 [768, 768], P(None, 'tensor')
- grad_w_value: float32 [768, 768], P(None, 'tensor')
- grad_b_value: float32 [768], P('tensor')
- grad_w_out: float32 [768, 768], P('tensor')
- grad_b_out: float32 [768], P('tensor')
- grad_gain_one: float32 [768], P('tensor')
- grad_shift_one: float32 [768], P('tensor')
- grad_w_up: float32 [768, 3072], P(None, 'tensor')
- grad_b_up: float32 [3072], P('tensor')
- grad_w_down: float32 [3072, 768], P('tensor')
- grad_b_down: float32 [768], P('tensor')
- grad_gain_two: float32 [768], P('tensor')
- grad_shift_two: float32 [768], P('tensor')
Inputs may be any that keep to these rules, and one draw needn't show every extreme that they name: Valid tokens of each sequence; the first lengths entries of a sequence's 1024 slots hold its tokens, and some sequence fills all 1024. `order`: a permutation of the 16 sequences.
All inputs are finite; a program needn't handle non-finite values.
Results may differ from a plain program's by a relative error of at most 0.015.
The roundings to bfloat16 on the way count: a program that leaves them out, or rounds other values in their place, can miss the bound.
Values may be sent and summed in bfloat16 or wider, within the bound.
No kernel may reach another device: no remote copies, remote signals or barrier semaphores. Data moves between devices by JAX's collectives and lax.ppermute only.
A program may use at most 192 MiB of HBM per device.

v0:
```python
import jax
import jax.numpy as jnp
from jax import lax
from jax.sharding import PartitionSpec as P

HEAD_DIM = 64


epsilon = 1e-06
masked_score = -1e30


def layer_norm(value, gain, shift):
    center = value - jnp.mean(value, axis=-1, keepdims=True)
    spread = jnp.mean(center * center, axis=-1, keepdims=True)
    return center * lax.rsqrt(spread + epsilon) * gain + shift


def gelu_exact(value):
    return jax.nn.gelu(value, approximate=False)


def product(left, right, form):
    return jnp.einsum(form, left, right, preferred_element_type=jnp.float32)


def masked_scores(query, keys, length):
    span = query.shape[0]
    scores = product(query, keys, "qhd,khd->hqk") * query.shape[-1] ** (-0.5)
    valid = jnp.arange(span) < length
    return jnp.where(valid[None, None, :], scores, masked_score)


def attend_forward(packed):
    query, keys, values, length = packed
    scores = masked_scores(query, keys, length)
    top = jnp.max(scores, axis=-1, keepdims=True)
    weights = jnp.exp(scores - top)
    total = jnp.sum(weights, axis=-1, keepdims=True)
    probs_low = (weights / total).astype(jnp.bfloat16)
    mixed = product(probs_low, values, "hqk,khd->qhd")
    return (mixed, (top + jnp.log(total))[..., 0])


def attend_backward(packed):
    query, keys, values, length, log_total, grad_mixed = packed
    scale = query.shape[-1] ** (-0.5)
    scores = masked_scores(query, keys, length)
    probs = jnp.exp(scores - log_total[..., None])
    grad_values = product(probs.astype(jnp.bfloat16), grad_mixed, "hqk,qhd->khd")
    grad_probs = product(grad_mixed, values, "qhd,khd->hqk")
    inner = jnp.sum(grad_probs * probs, axis=-1, keepdims=True)
    grad_scores = (probs * (grad_probs - inner) * scale).astype(jnp.bfloat16)
    grad_query = product(grad_scores, keys, "hqk,khd->qhd")
    grad_keys = product(grad_scores, query, "hqk,qhd->khd")
    return (grad_query, grad_keys, grad_values)


def on_device(
    inputs,
    lengths,
    order,
    w_query,
    b_query,
    w_key,
    w_value,
    b_value,
    w_out,
    b_out,
    gain_one,
    shift_one,
    w_up,
    b_up,
    w_down,
    b_down,
    gain_two,
    shift_two,
    cotangent,
):
    dp_count = lax.axis_size("dp")
    seq_local = inputs.shape[0] // dp_count
    seq_len = inputs.shape[1] * dp_count
    half = seq_len // lax.axis_size("tensor")
    offset = lax.axis_index("tensor") * half
    width = w_query.shape[0]
    local_width = w_query.shape[1]
    local_heads = local_width // HEAD_DIM
    token_count = seq_local * seq_len
    head_shape = (seq_local, seq_len, local_heads, HEAD_DIM)
    factor = (order.shape[0] * seq_len) ** (-0.5)
    arranged = inputs[order]
    vectors = jnp.stack([b_out, gain_one, shift_one, b_down, gain_two, shift_two])[None]
    dealt_half = lax.all_to_all(arranged, "dp", split_axis=0, concat_axis=1, tiled=True)
    dealt, vectors_full = (
        lax.all_gather(dealt_half, "tensor", axis=2, tiled=True),
        lax.all_gather(vectors, "tensor", axis=2, tiled=True),
    )
    vectors_full = vectors_full[0].astype(jnp.float32)
    bias_out = vectors_full[0]
    gain_first = vectors_full[1]
    shift_first = vectors_full[2]
    bias_down = vectors_full[3]
    gain_second = vectors_full[4]
    shift_second = vectors_full[5]
    dealt_lengths = lax.dynamic_slice_in_dim(
        lengths[order], lax.axis_index("dp") * seq_local, seq_local
    )
    tokens_flat = dealt.reshape(token_count, width)
    query = (product(tokens_flat, w_query, "nd,df->nf") + b_query.astype(jnp.float32)).astype(
        jnp.bfloat16
    )
    keys = product(tokens_flat, w_key, "nd,df->nf").astype(jnp.bfloat16)
    values = (product(tokens_flat, w_value, "nd,df->nf") + b_value.astype(jnp.float32)).astype(
        jnp.bfloat16
    )
    query_heads = query.reshape(head_shape)
    key_heads = keys.reshape(head_shape)
    value_heads = values.reshape(head_shape)
    mixed, log_total = lax.map(attend_forward, (query_heads, key_heads, value_heads, dealt_lengths))
    mixed = mixed.astype(jnp.bfloat16).reshape(token_count, local_width)
    attention = product(mixed, w_out, "nh,hd->nd").reshape(seq_local, seq_len, width)
    attention = lax.psum_scatter(attention, "tensor", scatter_dimension=1, tiled=True)
    residual = lax.dynamic_slice_in_dim(dealt, offset, half, 1).astype(jnp.float32)
    normed, norm_one_back = jax.vjp(
        layer_norm, residual + attention + bias_out, gain_first, shift_first
    )
    normed_low = normed.astype(jnp.bfloat16)
    normed_all = lax.all_gather(normed_low, "tensor", axis=1, tiled=True)
    normed_rows = normed_all.reshape(token_count, width)
    upper = product(normed_rows, w_up, "nd,df->nf") + b_up.astype(jnp.float32)
    active, gelu_back = jax.vjp(gelu_exact, upper)
    active_low = active.astype(jnp.bfloat16)
    feed_terms = product(active_low, w_down, "nf,fd->nd").reshape(seq_local, seq_len, width)
    feed = lax.psum_scatter(feed_terms, "tensor", scatter_dimension=1, tiled=True)
    result, norm_two_back = jax.vjp(
        layer_norm, normed + feed + bias_down, gain_second, shift_second
    )
    output = result.astype(jnp.bfloat16)
    grad_two, grad_gain_two, grad_shift_two = norm_two_back(cotangent.astype(jnp.float32))
    grad_bias_down = jnp.sum(grad_two, axis=(0, 1))
    grad_two_low = grad_two.astype(jnp.bfloat16)
    grad_all = lax.all_gather(grad_two_low, "tensor", axis=1, tiled=True)
    grad_rows = grad_all.reshape(token_count, width)
    grad_active = product(grad_rows, w_down, "nd,fd->nf")
    (grad_upper,) = gelu_back(grad_active)
    grad_upper_low = grad_upper.astype(jnp.bfloat16)
    grad_w_up = product(normed_rows, grad_upper_low, "nd,nf->df")
    grad_b_up = jnp.sum(grad_upper, axis=0)
    grad_w_down = product(active_low, grad_rows, "nf,nd->fd")
    normed_terms = product(grad_upper_low, w_up, "nf,df->nd").reshape(seq_local, seq_len, width)
    grad_normed = lax.psum_scatter(normed_terms, "tensor", scatter_dimension=1, tiled=True)
    grad_one, grad_gain_one, grad_shift_one = norm_one_back(grad_normed + grad_two)
    grad_bias_out = jnp.sum(grad_one, axis=(0, 1))
    grad_one_all = lax.all_gather(
        grad_one.astype(jnp.bfloat16), "tensor", axis=1, tiled=True
    ).reshape(token_count, width)
    grad_w_out = product(mixed, grad_one_all, "nh,nd->hd")
    grad_mixed = product(grad_one_all, w_out, "nd,hd->nh").astype(jnp.bfloat16).reshape(head_shape)
    grad_query, grad_keys, grad_values = lax.map(
        attend_backward, (query_heads, key_heads, value_heads, dealt_lengths, log_total, grad_mixed)
    )
    grad_query = grad_query.astype(jnp.bfloat16).reshape(token_count, local_width)
    grad_keys = grad_keys.astype(jnp.bfloat16).reshape(token_count, local_width)
    grad_values = grad_values.astype(jnp.bfloat16).reshape(token_count, local_width)
    grad_w_query = product(tokens_flat, grad_query, "nd,nf->df")
    grad_b_query = jnp.sum(grad_query, axis=0, dtype=jnp.float32)
    grad_w_key = product(tokens_flat, grad_keys, "nd,nf->df")
    grad_w_value = product(tokens_flat, grad_values, "nd,nf->df")
    grad_b_value = jnp.sum(grad_values, axis=0, dtype=jnp.float32)
    grad_inputs = (
        product(grad_query, w_query, "nf,df->nd")
        + product(grad_keys, w_key, "nf,df->nd")
        + product(grad_values, w_value, "nf,df->nd")
    )
    grad_inputs = grad_inputs.reshape(seq_local, seq_len, width)
    own_rows = lax.dynamic_slice_in_dim(grad_inputs, offset, half, 1) + grad_one
    grad_inputs = lax.dynamic_update_slice_in_dim(grad_inputs, own_rows, offset, 1)
    vector_grads = jnp.stack(
        [
            grad_bias_out,
            grad_gain_one,
            grad_shift_one,
            grad_bias_down,
            grad_gain_two,
            grad_shift_two,
        ]
    )[None]
    grad_inputs, vector_grads = (
        lax.psum_scatter(
            grad_inputs.astype(jnp.bfloat16), "tensor", scatter_dimension=2, tiled=True
        ).astype(jnp.float32),
        lax.psum_scatter(
            vector_grads.astype(jnp.bfloat16), "tensor", scatter_dimension=2, tiled=True
        ).astype(jnp.float32),
    )
    returned = lax.all_to_all(
        grad_inputs.astype(jnp.bfloat16), "dp", split_axis=1, concat_axis=0, tiled=True
    )
    inverse = jnp.zeros_like(order).at[order].set(jnp.arange(order.shape[0], dtype=jnp.int32))
    input_grad = returned[inverse]
    summed = lax.psum(
        (
            grad_w_query,
            grad_b_query,
            grad_w_key,
            grad_w_value,
            grad_b_value,
            grad_w_out,
            grad_w_up,
            grad_b_up,
            grad_w_down,
            vector_grads,
        ),
        "dp",
    )
    vector_sums = summed[9][0] * factor
    return (
        output,
        input_grad,
        summed[0] * factor,
        summed[1] * factor,
        summed[2] * factor,
        summed[3] * factor,
        summed[4] * factor,
        summed[5] * factor,
        vector_sums[0],
        vector_sums[1],
        vector_sums[2],
        summed[6] * factor,
        summed[7] * factor,
        summed[8] * factor,
        vector_sums[3],
        vector_sums[4],
        vector_sums[5],
    )


def solution(mesh):
    return jax.shard_map(
        on_device,
        mesh=mesh,
        in_specs=(
            P(None, "dp", "tensor"),
            P(),
            P(),
            P(None, "tensor"),
            P("tensor"),
            P(None, "tensor"),
            P(None, "tensor"),
            P("tensor"),
            P("tensor", None),
            P("tensor"),
            P("tensor"),
            P("tensor"),
            P(None, "tensor"),
            P("tensor"),
            P("tensor", None),
            P("tensor"),
            P("tensor"),
            P("tensor"),
            P("dp", "tensor", None),
        ),
        out_specs=(
            P("dp", "tensor", None),
            P(None, "dp", "tensor"),
            P(None, "tensor"),
            P("tensor"),
            P(None, "tensor"),
            P(None, "tensor"),
            P("tensor"),
            P("tensor", None),
            P("tensor"),
            P("tensor"),
            P("tensor"),
            P(None, "tensor"),
            P("tensor"),
            P("tensor", None),
            P("tensor"),
            P("tensor"),
            P("tensor"),
        ),
        check_vma=False,
    )
```

profile of v0, /device:TPU:0, one launch (start us, length us, event | category | flops | bytes accessed | tf_op | source)
XLA Modules:
  0.0 789.3 jit_solution(8190659484800640758)
XLA Ops:
  8.6 1.8 gather_fusion
  10.5 29.5 %all_to_all.24 = bf16[16,64,384]{2,1,0:T(8,128)(2,1)} all-to-all(bf16[16,64,384]{2,1,0:T(8,128)(2,1)S(1)} %gather_fusion), channel_id=1, replica_groups=mesh['dp'=16,'tensor'=2] {'dp'}, dimensions={0} | all-to-all | bytes 1572864 | tf_op jit(solution)/shard_map/all_to_all | solution.py:93
  42.0 5.6 all-gather.6.cloned.1.call-done
  47.7 2.5 fusion.79
  51.0 10.6 %fusion.3 = (f32[6,1024]{1,0:T(8,128)S(1)}, f32[6,1024,1024]{1,2,0:T(8,128)}) fusion(pred[1024]{0:T(1024)(128)(4,1)S(1)} %iota_compare_fusion, bf16[1024,6,64]{0,2,1:T(8,128)(2,1)S(1)} %bitcast.140, bf16[1024,6,64]{0,2,1:T(8,128)(2,1)S(1)} %bitcast.138), kind=kOutput, calls=%fused_computation.13 | convolution fusion | flops 824174592 | bytes 26764288 | tf_op jit(solution)/shard_map/while/body/eval_jaxpr/qhd,khd->hqk/dot_general | solution.py:24
  61.6 11.8 %fusion.2 = f32[6,1024]{1,0:T(8,128)S(1)} fusion(f32[6,1024,1024]{1,2,0:T(8,128)} %get-tuple-element.112, f32[6,1024]{1,0:T(8,128)S(1)} %get-tuple-element.111, pred[1024]{0:T(1024)(128)(4,1)S(1)} %iota_compare_fusion), kind=kLoop, calls=%fused_computation.12 | loop fusion | flops 25159680 | bytes 25216000 | tf_op jit(solution)/shard_map/while/body/eval_jaxpr/reduce_sum | solution.py:39
  74.3 11.8 %fusion.91 = bf16[6,64,1024]{2,1,0:T(8,128)(2,1)S(1)} fusion(bf16[1024,6,64]{0,2,1:T(8,128)(2,1)S(1)} %bitcast.134, f32[6,1024,1024]{1,2,0:T(8,128)} %get-tuple-element.112, f32[6,1024]{1,0:T(8,128)S(1)} %fusion.2, f32[6,1024]{1,0:T(8,128)S(1)} %get-tuple-element.111, pred[1024]{0:T(1024)(128)(4,1)S(1)} %iota_compare_fusion), kind=kOutput, calls=%fused_computation.106 | convolution fusion | flops 837156864 | bytes 26788864 | tf_op jit(solution)/shard_map/while/body/eval_jaxpr/hqk,khd->qhd/dot_general | solution.py:24
  87.0 2.7 convolution_bitcast_fusion.2
  90.0 2.0 all-gather
  92.1 10.2 %reduce-scatter.10.cloned.1.call-done = f32[1,512,768]{2,1,0:T(8,128)} async-done(((f32[1,1024,768]{2,1,0:T(8,128)}), f32[1,512,768]{2,1,0:T(8,128)}) %reduce-scatter.10.cloned.1.call-update) | async-done | bytes 1572880 | tf_op jit(solution)/shard_map/reduce_scatter | solution.py:122
  102.2 1.9 fusion.115
  106.6 11.2 %all-gather.8.cloned.1.call-done = bf16[1,1024,768]{2,1,0:T(8,128)(2,1)} async-done(((bf16[1,512,768]{2,1,0:T(8,128)(2,1)}), bf16[1,1024,768]{2,1,0:T(8,128)(2,1)}) %all-gather.8.cloned.1.call-update) | async-done | bytes 1572880 | tf_op jit(solution)/shard_map/all_gather | solution.py:128
  117.7 18.2 %multiply_convert_fusion.1 = (bf16[1024,1536]{1,0:T(8,128)(2,1)S(1)}, f32[1024,1536]{1,0:T(8,128)}, f32[1024,1536]{1,0:T(8,128)}) fusion(f32[1536]{0:T(1024)S(1)} %convert_element_type.127, bf16[768,1536]{1,0:T(8,128)(2,1)S(1)} %copy-done, bf16[1,1024,768]{2,1,0:T(8,128)(2,1)} %all-gather.8.cloned.1.call-done), kind=kOutput, calls=%fused_computation.31 | convolution fusion | flops 2519728128 | bytes 19666944 | tf_op jit(solution)/shard_map/nd,df->nf/dot_general | solution.py:24
  136.0 1.6 copy-done.48
  137.6 4.3 convolution_bitcast_fusion.1
  141.9 12.4 %reduce-scatter.12.cloned.1.call-done = f32[1,512,768]{2,1,0:T(8,128)} async-done(((f32[1,1024,768]{2,1,0:T(8,128)}), f32[1,512,768]{2,1,0:T(8,128)}) %reduce-scatter.12.cloned.1.call-update) | async-done | bytes 1572880 | tf_op jit(solution)/shard_map/reduce_scatter | solution.py:134
  154.4 2.5 fusion.113
  162.3 10.8 %all-gather.10.cloned.1.call-done = bf16[1,1024,768]{2,1,0:T(8,128)(2,1)} async-done(((bf16[1,512,768]{2,1,0:T(8,128)(2,1)}), bf16[1,1024,768]{2,1,0:T(8,128)(2,1)}) %all-gather.10.cloned.1.call-update) | async-done | bytes 1572880 | tf_op jit(solution)/shard_map/all_gather | solution.py:142
  173.1 10.2 %fusion.118 = (f32[1536]{0:T(1024)S(1)}, bf16[1024,1536]{1,0:T(8,128)(2,1)S(1)}) fusion(f32[1024,1536]{1,0:T(8,128)} %get-tuple-element.103, bf16[1536,768]{1,0:T(8,128)(2,1)} %param.33, bf16[1,1024,768]{2,1,0:T(8,128)(2,1)} %all-gather.10.cloned.1.call-done, f32[1024,1536]{1,0:T(8,128)} %get-tuple-element.113, f32[1536]{0:T(1024)S(1)} %convert_element_type.127), kind=kOutput, calls=%fused_computation.168 | convolution fusion | flops 2441083392 | bytes 19673088 | tf_op jit(solution)/shard_map/nd,fd->nf/dot_general | solution.py:24
  183.3 1.6 copy-done.10
  184.9 4.3 convolution_bitcast_fusion
  189.3 12.4 %reduce-scatter.14.cloned.1.call-done = f32[1,512,768]{2,1,0:T(8,128)} async-done(((f32[1,1024,768]{2,1,0:T(8,128)}), f32[1,512,768]{2,1,0:T(8,128)}) %reduce-scatter.14.cloned.1.call-update) | async-done | bytes 1572880 | tf_op jit(solution)/shard_map/reduce_scatter | solution.py:151
  201.8 2.7 multiply_reduce_fusion.1
  207.4 11.2 %all-gather.12.cloned.1.call-done = bf16[1,1024,768]{2,1,0:T(8,128)(2,1)} async-done(((bf16[1,512,768]{2,1,0:T(8,128)(2,1)}), bf16[1,1024,768]{2,1,0:T(8,128)(2,1)}) %all-gather.12.cloned.1.call-update) | async-done | bytes 1572880 | tf_op jit(solution)/shard_map/all_gather | solution.py:154
  218.6 2.2 fusion.82
  220.8 10.2 %fusion.119 = f32[6,1024,1024]{1,2,0:T(8,128)} fusion(bf16[1024,6,64]{0,2,1:T(8,128)(2,1)S(1)} %bitcast.136, bf16[1024,6,64]{0,2,1:T(8,128)(2,1)S(1)} %bitcast.135), kind=kOutput, calls=%fused_computation.169 | convolution fusion | flops 805306368 | bytes 26738688 | tf_op jit(solution)/shard_map/while/body/eval_jaxpr/qhd,khd->hqk/dot_general | solution.py:24
  231.1 12.3 %convert_reduce_fusion = (f32[6,64]{1,0:T(8,128)S(1)}, bf16[6,64,1024]{2,1,0:T(8,128)(2,1)}) fusion(bf16[1024,6,64]{0,2,1:T(8,128)(2,1)S(1)} %bitcast.137, f32[6,1024,1024]{1,2,0:T(8,128)} %get-tuple-element.112, f32[6,1024]{1,0:T(8,128)S(1)} %log_add_fusion, pred[1024]{0:T(1024)(128)(4,1)S(1)} %iota_compare_fusion), kind=kOutput, calls=%fused_computation.88 | convolution fusion | flops 831651456 | bytes 26765824 | tf_op jit(solution)/shard_map/while/body/eval_jaxpr/hqk,qhd->khd/dot_general | solution.py:24
  243.4 34.1 %fusion.88 = bf16[6,64,1024]{2,1,0:T(8,128)(2,1)S(1)} fusion(bf16[1024,6,64]{0,2,1:T(8,128)(2,1)S(1)} %bitcast.141, f32[6,1024,1024]{1,2,0:T(8,128)} %fusion.119, f32[6,1024,1024]{1,2,0:T(8,128)} %get-tuple-element.112, f32[6,1024]{1,0:T(8,128)S(1)} %log_add_fusion, pred[1024]{0:T(1024)(128)(4,1)S(1)} %iota_compare_fusion), kind=kOutput, calls=%fused_computation.105 | convolution fusion | flops 874912768 | bytes 51930112 | tf_op jit(solution)/shard_map/while/body/eval_jaxpr/hqk,qhd->khd/dot_general | solution.py:24
  277.6 34.3 %convert_reduce_fusion.1 = (f32[6,64]{1,0:T(8,128)S(1)}, bf16[6,64,1024]{2,1,0:T(8,128)(2,1)S(1)}) fusion(bf16[1024,6,64]{0,2,1:T(8,128)(2,1)S(1)} %bitcast.139, f32[6,1024,1024]{1,2,0:T(8,128)} %fusion.119, f32[6,1024,1024]{1,2,0:T(8,128)} %get-tuple-element.112, f32[6,1024]{1,0:T(8,128)S(1)} %log_add_fusion, pred[1024]{0:T(1024)(128)(4,1)S(1)} %iota_compare_fusion), kind=kOutput, calls=%fused_computation.89 | convolution fusion | flops 875698816 | bytes 51931648 | tf_op jit(solution)/shard_map/while/body/eval_jaxpr/hqk,khd->qhd/dot_general | solution.py:24
  311.9 2.4 fusion.121
  318.5 5.6 copy.58
  324.1 3.6 copy.68
  328.0 7.4 fusion.48
  335.4 4.3 fusion.54
  341.3 3.2 fusion.44
  344.5 3.6 fusion.58
  348.1 2.0 fusion.62
  350.1 2.0 fusion.60
  352.2 3.1 reshape_bitcast_fusion
  355.3 5.0 copy.53
  360.9 5.4 reduce.43
  367.4 6.8 all-to-all-start.1
  376.3 98.0 %all-reduce = (f32[384]{0:T(512)S(1)}, f32[384]{0:T(512)S(1)}, f32[1,6,384]{2,1,0:T(8,128)S(1)}, f32[1536]{0:T(1024)S(1)}) all-reduce(f32[384]{0:T(512)S(1)} %reduce_sum.220, f32[384]{0:T(512)S(1)} %reduce_sum.222, bf16[1,6,384]{2,1,0:T(8,128)(2,1)S(1)} %copy.61, ...), channel_id=1, replica_groups=mesh['dp'=16,'tensor'=2] {'dp'}, use_global_device_ids=true, to_apply=%region_18.19 | all-reduce | flops 4608 | bytes 32256 | tf_op jit(solution)/shard_map/psum | solution.py:201
  478.5 290.0 %all-reduce.4.cloned.1.call-done = (f32[768,384]{1,0:T(8,128)}, f32[768,384]{1,0:T(8,128)}, f32[768,384]{1,0:T(8,128)}, f32[384,768]{1,0:T(8,128)}, f32[768,1536]{1,0:T(8,128)}, /*index=5*/f32[1536,768]{1,0:T(8,128)}) async-done(((f32[768,384]{1,0:T(8,128)}, f32[768,384]{1,0:T(8,128)}, f32[768,384]{1,0:T(8,128)}, f32[384,768]{1,0:T(8,128)}, f32[768,1536]{1,0:T(8,128)}, /*index=5*/f32[1536,768]{1,0:T(8,128)}), ...) | async-done | bytes 14155792 | tf_op jit(solution)/shard_map/psum | solution.py:201
  768.5 2.5 broadcast_multiply_fusion.5
  771.0 2.4 broadcast_multiply_fusion.2
  773.3 2.9 broadcast_multiply_fusion.1
  777.4 2.7 broadcast_multiply_fusion
  (193 shorter events, 33.8 us)
Async XLA Ops:
  7.2 110.5 %copy-start = (bf16[768,1536]{1,0:T(8,128)(2,1)S(1)}, bf16[768,1536]{1,0:T(8,128)(2,1)}, u32[]{:S(2)}) copy-start(bf16[768,1536]{1,0:T(8,128)(2,1)} %param.31) | copy-start | bytes 7077892
  7.2 32.9 %copy-start.38 = (bf16[384]{0:T(512)(128)(2,1)S(1)}, bf16[384]{0:T(512)(128)(2,1)}, u32[]{:S(2)}) copy-start(bf16[384]{0:T(512)(128)(2,1)} %param.23) | copy-start | bytes 2308
  7.2 32.9 %copy-start.39 = (bf16[384]{0:T(512)(128)(2,1)S(1)}, bf16[384]{0:T(512)(128)(2,1)}, u32[]{:S(2)}) copy-start(bf16[384]{0:T(512)(128)(2,1)} %param.26) | copy-start | bytes 2308
  7.2 32.9 %copy-start.2 = (s32[16]{0:T(128)S(1)}, s32[16]{0:T(128)}, u32[]{:S(2)}) copy-start(s32[16]{0:T(128)} %param.20) | copy-start | bytes 196
  7.2 40.4 %all-gather.6.cloned.1.call-start = ((), (), s32[]{:S(2)}) async-start(), calls=%async_computation.7 | async-start | bytes 2359296 | tf_op jit(solution)/shard_map/all_gather | solution.py:95
  40.0 10.2 %copy-start.31 = (bf16[768,384]{1,0:T(8,128)(2,1)S(1)}, bf16[768,384]{1,0:T(8,128)(2,1)}, u32[]{:S(2)}) copy-start(bf16[768,384]{1,0:T(8,128)(2,1)} %param.22) | copy-start | bytes 1769476
  40.0 62.2 %reduce-scatter.10.cloned.1.call-start = ((), (), s32[]{:S(2)}) async-start(), calls=%async_computation.8 | async-start | bytes 4718592 | tf_op jit(solution)/shard_map/reduce_scatter | solution.py:122
  50.2 11.5 %copy-start.15 = (bf16[1024,384]{0,1:T(8,128)(2,1)}, bf16[1024,384]{0,1:T(8,128)(2,1)S(1)}, u32[]{:S(2)}) copy-start(bf16[1024,384]{0,1:T(8,128)(2,1)S(1)} %fusion.79) | copy-start | bytes 2359300
  51.0 10.6 %copy-start.17 = (bf16[1024,384]{0,1:T(8,128)(2,1)}, bf16[1024,384]{0,1:T(8,128)(2,1)S(1)}, u32[]{:S(2)}) copy-start(bf16[1024,384]{0,1:T(8,128)(2,1)S(1)} %add_convert_fusion.1) | copy-start | bytes 2359300
  61.6 11.8 %copy-start.33 = (bf16[768,384]{1,0:T(8,128)(2,1)S(1)}, bf16[768,384]{1,0:T(8,128)(2,1)}, u32[]{:S(2)}) copy-start(bf16[768,384]{1,0:T(8,128)(2,1)} %param.25) | copy-start | bytes 1769476
  74.2 11.9 %copy-start.13 = (bf16[1024,384]{0,1:T(8,128)(2,1)}, bf16[1024,384]{0,1:T(8,128)(2,1)S(1)}, u32[]{:S(2)}) copy-start(bf16[1024,384]{0,1:T(8,128)(2,1)S(1)} %add_convert_fusion.2) | copy-start | bytes 2359300
  74.3 12.7 %copy-start.29 = (bf16[384,768]{1,0:T(8,128)(2,1)S(1)}, bf16[384,768]{1,0:T(8,128)(2,1)}, u32[]{:S(2)}) copy-start(bf16[384,768]{1,0:T(8,128)(2,1)} %param.27) | copy-start | bytes 1769476
  87.0 2.8 copy-start.40
  87.0 2.8 copy-start.41
  87.0 2.8 copy-start.42
  87.0 2.9 copy-start.43
  87.0 2.9 copy-start.44
  87.0 2.9 copy-start.45
  89.8 28.0 %all-gather.8.cloned.1.call-start = ((), (), s32[]{:S(2)}) async-start(), calls=%async_computation.9 | async-start | bytes 2359296 | tf_op jit(solution)/shard_map/all_gather | solution.py:128
  106.5 47.9 %reduce-scatter.12.cloned.1.call-start = ((), (), s32[]{:S(2)}) async-start(), calls=%async_computation.10 | async-start | bytes 4718592 | tf_op jit(solution)/shard_map/reduce_scatter | solution.py:134
  117.7 19.9 %copy-start.47 = (bf16[1536,768]{1,0:T(8,128)(2,1)S(1)}, bf16[1536,768]{1,0:T(8,128)(2,1)}, u32[]{:S(2)}) copy-start(bf16[1536,768]{1,0:T(8,128)(2,1)} %param.33) | copy-start | bytes 7077892
  141.9 31.2 %all-gather.10.cloned.1.call-start = ((), (), s32[]{:S(2)}) async-start(), calls=%async_computation.11 | async-start | bytes 2359296 | tf_op jit(solution)/shard_map/all_gather | solution.py:142
  154.4 2.8 copy-start.8
  161.8 39.9 %reduce-scatter.14.cloned.1.call-start = ((), (), s32[]{:S(2)}) async-start(), calls=%async_computation.12 | async-start | bytes 4718592 | tf_op jit(solution)/shard_map/reduce_scatter | solution.py:151
  189.2 12.5 %copy-start.4 = (f32[1,512,768]{2,1,0:T(8,128)S(1)}, f32[1,512,768]{2,1,0:T(8,128)}, u32[]{:S(2)}) copy-start(f32[1,512,768]{2,1,0:T(8,128)} %copy-done.3) | copy-start | bytes 4718596
  189.3 29.3 %all-gather.12.cloned.1.call-start = ((), (), s32[]{:S(2)}) async-start(), calls=%async_computation.13 | async-start | bytes 2359296 | tf_op jit(solution)/shard_map/all_gather | solution.py:154
  204.5 14.1 %copy-start.30 = (bf16[384,768]{1,0:T(8,128)(2,1)S(1)}, bf16[384,768]{1,0:T(8,128)(2,1)}, u32[]{:S(2)}) copy-start(bf16[384,768]{1,0:T(8,128)(2,1)} %param.27) | copy-start | bytes 1769476
  206.3 14.6 %copy-start.14 = (bf16[1024,384]{0,1:T(8,128)(2,1)S(1)}, bf16[1024,384]{0,1:T(8,128)(2,1)}, u32[]{:S(2)}) copy-start(bf16[1024,384]{0,1:T(8,128)(2,1)} %copy-done.13) | copy-start | bytes 2359300
  207.4 144.8 %reduce-scatter.16.cloned.1.call-start = ((), (), s32[]{:S(2)}) async-start(), calls=%async_computation.14 | async-start | bytes 2359296
  231.1 12.4 %copy-start.18 = (bf16[1024,384]{0,1:T(8,128)(2,1)S(1)}, bf16[1024,384]{0,1:T(8,128)(2,1)}, u32[]{:S(2)}) copy-start(bf16[1024,384]{0,1:T(8,128)(2,1)} %copy-done.17) | copy-start | bytes 2359300
  243.4 34.2 %copy-start.16 = (bf16[1024,384]{0,1:T(8,128)(2,1)S(1)}, bf16[1024,384]{0,1:T(8,128)(2,1)}, u32[]{:S(2)}) copy-start(bf16[1024,384]{0,1:T(8,128)(2,1)} %copy-done.15) | copy-start | bytes 2359300
  277.6 34.3 %copy-start.23 = (bf16[6,64,1024]{2,1,0:T(8,128)(2,1)}, bf16[6,64,1024]{2,1,0:T(8,128)(2,1)S(1)}, u32[]{:S(2)}) copy-start(bf16[6,64,1024]{2,1,0:T(8,128)(2,1)S(1)} %fusion.88) | copy-start | bytes 2359300
  311.9 3.5 copy-start.25
  327.8 47.2 %reduce-scatter.18.cloned.1.call-start = ((), (), s32[]{:S(2)}) async-start(), calls=%async_computation.15 | async-start | bytes 294912
  328.0 7.4 copy-start.11
  328.0 7.4 copy-start.12
  335.4 5.9 copy-start.22
  339.8 4.7 copy-start.28
  341.0 427.5 %all-reduce.4.cloned.1.call-start = ((), (), s32[]{:S(2)}) async-start(), calls=%async_computation.16 | async-start | bytes 28311552 | tf_op jit(solution)/shard_map/psum | solution.py:201
  344.5 3.6 copy-start.26
  344.5 3.6 copy-start.36
  367.4 108.7 %all-to-all-start.1 = ((bf16[16,2,12288]{2,1,0:T(2,128)(2,1)}), bf16[16,2,12288]{2,1,0:T(2,128)(2,1)S(1)}, u32[]{:S(2)}, u32[]{:S(2)}) async-start(bf16[16,2,12288]{2,1,0:T(2,128)(2,1)} %reshape.457), calls=%async_computation.4 | async-start | bytes 1572864 | tf_op jit(solution)/shard_map/all_to_all | solution.py:196
  768.5 4.9 copy-start.9
  773.3 3.9 slice-start
  773.3 4.0 slice-start.1
  777.3 2.7 copy-start.19
  777.3 2.7 copy-start.20
  777.4 4.7 copy-start.1
  (14 other events, 21.3 us)
Sparse Core Ops, SparseCore 0:
  40.1 7.4 all-gather.5
  89.9 12.3 reduce-scatter.9
  106.6 11.0 all-gather.7
  142.0 12.3 reduce-scatter.11
  162.0 11.0 all-gather.9
  189.4 12.3 reduce-scatter.13
  207.5 11.0 all-gather.11
  327.9 10.2 reduce-scatter.15
  341.1 8.8 reduce-scatter.17
  357.4 411.0 all-reduce.3
where the time goes:
time: 798 us; the launch traced here: 789 us
  waiting for transfers between devices  364 us (46%)
  matrix products  186 us (23%)
  blocking collectives  130 us (16%)
  other arithmetic  46.5 us (6%)
  local copies, waits for them, and re-layouts  39.5 us (5%)
  between operations  15.4 us (2%)
    psum x1, waiting for transfers between devices, on_device(): lax.psum((grad_w_query, grad_b_query, grad_w_key, grad_w_value, grad_b_va...  290 us
    dot_general x24, matrix products, product(): return jnp.einsum(form, left, right, preferred_element_type=jnp.float32)  186 us
    psum x1, blocking collectives, on_device(): lax.psum((grad_w_query, grad_b_query, grad_w_key, grad_w_value, grad_b_va...  98 us
    all_to_all x1, blocking collectives, on_device(): lax.all_to_all(arranged, 'dp', split_axis=0, concat_axis=1, tiled=True)  29.5 us
    unnamed x114, local copies, waits for them, and re-layouts  28.1 us
  transfers between devices with their start and end apart: 11, of which 8 were waited for; matrix products, arithmetic and copies ran while one was open for 6% of the time, Pallas kernels for 0%

commit v1 on v0

v1 whole, which is shorter than its diff:
```python
import jax
import jax.numpy as jnp
from jax import lax
from jax.sharding import PartitionSpec as P

HEAD_DIM = 64
epsilon = 1e-06
masked_score = -1e30
f32 = jnp.float32
bf16 = jnp.bfloat16


def layer_norm(value, gain, shift):
    center = value - jnp.mean(value, axis=-1, keepdims=True)
    spread = jnp.mean(center * center, axis=-1, keepdims=True)
    return center * lax.rsqrt(spread + epsilon) * gain + shift


def gelu_exact(value):
    return jax.nn.gelu(value, approximate=False)


def product(left, right, form):
    return jnp.einsum(form, left, right, preferred_element_type=f32)


def masked_scores(query, keys, valid):
    scores = product(query, keys, "qhd,khd->hqk") * query.shape[-1] ** (-0.5)
    return jnp.where(valid[None, None, :], scores, masked_score)


def attend_forward(query, keys, values, valid):
    scores = masked_scores(query, keys, valid)
    top = jnp.max(scores, axis=-1, keepdims=True)
    weights = jnp.exp(scores - top)
    total = jnp.sum(weights, axis=-1, keepdims=True)
    probs_low = (weights / total).astype(bf16)
    mixed = product(probs_low, values, "hqk,khd->qhd")
    return mixed, (top + jnp.log(total))[..., 0]


def attend_backward(query, keys, values, valid, log_total, grad_mixed):
    scale = query.shape[-1] ** (-0.5)
    scores = masked_scores(query, keys, valid)
    probs = jnp.exp(scores - log_total[..., None])
    grad_values = product(probs.astype(bf16), grad_mixed, "hqk,qhd->khd")
    grad_probs = product(grad_mixed, values, "qhd,khd->hqk")
    inner = jnp.sum(grad_probs * probs, axis=-1, keepdims=True)
    grad_scores = (probs * (grad_probs - inner) * scale).astype(bf16)
    grad_query = product(grad_scores, keys, "hqk,khd->qhd")
    grad_keys = product(grad_scores, query, "hqk,qhd->khd")
    return grad_query, grad_keys, grad_values


def swap(value):
    return lax.ppermute(value, "tensor", [(0, 1), (1, 0)])


def across(value, bit):
    count = lax.axis_size("dp")
    return lax.ppermute(value, "dp", [(i, i ^ (1 << bit)) for i in range(count)])


def bit_of(bit):
    return (lax.axis_index("dp") >> bit) & 1


def bit_orders():
    bits = lax.axis_size("dp").bit_length() - 1
    plain = list(range(bits))
    other = [1, 0] + plain[2:]
    return plain, other


def scatter_sum(value, bits):
    for bit in bits:
        half = value.shape[0] // 2
        mine = bit_of(bit)
        away = lax.dynamic_slice_in_dim(value, (1 - mine) * half, half, 0).astype(bf16)
        kept = lax.dynamic_slice_in_dim(value, mine * half, half, 0)
        value = kept + across(away, bit).astype(f32)
    return value


def gather_back(value, bits):
    for bit in reversed(bits):
        mine = bit_of(bit)
        half = value.shape[0]
        got = across(value, bit)
        joined = jnp.zeros((2 * half,) + value.shape[1:], value.dtype)
        joined = lax.dynamic_update_slice_in_dim(joined, value, mine * half, 0)
        value = lax.dynamic_update_slice_in_dim(joined, got, (1 - mine) * half, 0)
    return value


def reduce_all(value, bits, factor):
    count = lax.axis_size("dp")
    rows, columns = value.shape
    parts = value.reshape(count, rows // count, columns)
    total = (scatter_sum(parts, bits) * factor).astype(bf16)
    return gather_back(total, bits).reshape(rows, columns).astype(f32)


def on_device(
    inputs,
    lengths,
    order,
    w_query,
    b_query,
    w_key,
    w_value,
    b_value,
    w_out,
    b_out,
    gain_one,
    shift_one,
    w_up,
    b_up,
    w_down,
    b_down,
    gain_two,
    shift_two,
    cotangent,
):
    dp_count = lax.axis_size("dp")
    seq_len = inputs.shape[1] * dp_count
    half = seq_len // 2
    side = lax.axis_index("tensor")
    width = w_query.shape[0]
    local_width = w_query.shape[1]
    local_heads = local_width // HEAD_DIM
    head_shape = (seq_len, local_heads, HEAD_DIM)
    factor = (order.shape[0] * seq_len) ** (-0.5)
    plain, other = bit_orders()

    def halves(value, axis):
        size = value.shape[axis] // 2
        mine = lax.dynamic_slice_in_dim(value, side * size, size, axis)
        theirs = lax.dynamic_slice_in_dim(value, (1 - side) * size, size, axis)
        return mine, theirs

    def ordered(mine, theirs, axis):
        return jnp.where(
            side == 0,
            jnp.concatenate([mine, theirs], axis),
            jnp.concatenate([theirs, mine], axis),
        )

    vectors = jnp.stack([b_out, gain_one, shift_one, b_down, gain_two, shift_two])
    vectors_full = ordered(vectors, swap(vectors), 1).astype(f32)
    bias_out, gain_first, shift_first, bias_down, gain_second, shift_second = [
        vectors_full[i] for i in range(6)
    ]
    dealt_half = lax.all_to_all(inputs[order], "dp", split_axis=0, concat_axis=1, tiled=True)[0]
    dealt = ordered(dealt_half, swap(dealt_half), 1)
    length = lengths[order][lax.axis_index("dp")]
    position = (jnp.arange(seq_len) + side * half) % seq_len
    valid = position < length
    own, rest = halves(dealt, 0)
    tokens = jnp.concatenate([own, rest], 0)

    query = (product(tokens, w_query, "nd,df->nf") + b_query.astype(f32)).astype(bf16)
    keys = product(tokens, w_key, "nd,df->nf").astype(bf16)
    values = (product(tokens, w_value, "nd,df->nf") + b_value.astype(f32)).astype(bf16)
    heads = [value.reshape(head_shape) for value in (query, keys, values)]
    mixed, log_total = attend_forward(*heads, valid)
    mixed = mixed.astype(bf16).reshape(seq_len, local_width)

    def join(terms_of):
        away = terms_of(1).astype(bf16)
        got = swap(away)
        return terms_of(0) + got.astype(f32)

    def rows_of(value, which):
        return value[which * half : (which + 1) * half]

    attention = join(lambda k: product(rows_of(mixed, k), w_out, "nh,hd->nd"))
    normed, norm_one_back = jax.vjp(
        layer_norm, own.astype(f32) + attention + bias_out, gain_first, shift_first
    )
    normed_low = normed.astype(bf16)
    normed_pair = [normed_low, swap(normed_low)]
    bias_up = b_up.astype(f32)
    active_pair, gelu_backs = [], []
    for part in normed_pair:
        upper = product(part, w_up, "nd,df->nf") + bias_up
        active, back = jax.vjp(gelu_exact, upper)
        active_pair.append(active.astype(bf16))
        gelu_backs.append(back)
    feed = join(lambda k: product(active_pair[k], w_down, "nf,fd->nd"))
    result, norm_two_back = jax.vjp(
        layer_norm, normed + feed + bias_down, gain_second, shift_second
    )
    output = result.astype(bf16)
    grad_two, grad_gain_two, grad_shift_two = norm_two_back(cotangent[0].astype(f32))
    grad_bias_down = jnp.sum(grad_two, axis=0)
    grad_two_low = grad_two.astype(bf16)
    grad_pair = [grad_two_low, swap(grad_two_low)]
    upper_pair, bias_up_terms = [], []
    for part, back in zip(grad_pair, gelu_backs):
        (grad_upper,) = back(product(part, w_down, "nd,fd->nf"))
        bias_up_terms.append(jnp.sum(grad_upper, axis=0))
        upper_pair.append(grad_upper.astype(bf16))
    grad_normed = join(lambda k: product(upper_pair[k], w_up, "nf,df->nd"))
    grad_w_down = product(
        jnp.concatenate(active_pair, 0), jnp.concatenate(grad_pair, 0), "nf,nd->fd"
    )
    down_sum = reduce_all(grad_w_down, plain, factor)
    grad_w_up = product(
        jnp.concatenate(normed_pair, 0), jnp.concatenate(upper_pair, 0), "nd,nf->df"
    )
    up_sum = reduce_all(grad_w_up, other, factor)
    grad_one, grad_gain_one, grad_shift_one = norm_one_back(grad_normed + grad_two)
    grad_bias_out = jnp.sum(grad_one, axis=0)
    grad_one_low = grad_one.astype(bf16)
    grad_one_all = jnp.concatenate([grad_one_low, swap(grad_one_low)], 0)
    grad_mixed = product(grad_one_all, w_out, "nd,hd->nh").astype(bf16)
    grad_w_out = product(mixed, grad_one_all, "nh,nd->hd")
    out_sum = reduce_all(grad_w_out, plain, factor)
    grad_query, grad_keys, grad_values = [
        value.astype(bf16).reshape(seq_len, local_width)
        for value in attend_backward(*heads, valid, log_total, grad_mixed.reshape(head_shape))
    ]

    def input_terms(which):
        pieces = [
            product(grad, halves(weight, 0)[which], "nf,df->nd")
            for grad, weight in (
                (grad_query, w_query),
                (grad_keys, w_key),
                (grad_values, w_value),
            )
        ]
        summed = pieces[0] + pieces[1] + pieces[2]
        straight = halves(grad_one, 1)[which]
        return jnp.concatenate([summed[:half] + straight, summed[half:]], 0)

    away = input_terms(1).astype(bf16)
    got = swap(away)
    kept = input_terms(0)
    grad_own = kept[:half] + got[half:].astype(f32)
    grad_rest = kept[half:] + got[:half].astype(f32)
    grad_inputs = ordered(grad_own.astype(bf16), grad_rest.astype(bf16), 0)[None]
    returned = lax.all_to_all(grad_inputs, "dp", split_axis=1, concat_axis=0, tiled=True)
    inverse = jnp.zeros_like(order).at[order].set(jnp.arange(order.shape[0], dtype=jnp.int32))
    input_grad = returned[inverse]

    grad_w_query = product(tokens, grad_query, "nd,nf->df")
    grad_w_key = product(tokens, grad_keys, "nd,nf->df")
    grad_w_value = product(tokens, grad_values, "nd,nf->df")
    query_sum = reduce_all(grad_w_query, plain, factor)
    key_sum = reduce_all(grad_w_key, other, factor)
    value_sum = reduce_all(grad_w_value, other, factor)

    vector_grads = jnp.stack(
        [
            grad_bias_out,
            grad_gain_one,
            grad_shift_one,
            grad_bias_down,
            grad_gain_two,
            grad_shift_two,
        ]
    )
    mine, theirs = halves(vector_grads, 1)
    mine = mine + swap(theirs)
    small = jnp.concatenate(
        [
            mine.reshape(-1),
            bias_up_terms[0] + bias_up_terms[1],
            jnp.sum(grad_query, axis=0, dtype=f32),
            jnp.sum(grad_values, axis=0, dtype=f32),
        ]
    ).reshape(-1, 128)
    for bit in plain:
        small = small + across(small, bit)
    small = (small * factor).reshape(-1)
    vector_sums = small[: 6 * local_width].reshape(6, local_width)
    b_up_sum = small[6 * local_width : 10 * local_width]
    b_query_sum = small[10 * local_width : 11 * local_width]
    b_value_sum = small[11 * local_width :]
    return (
        output[None],
        input_grad,
        query_sum,
        b_query_sum,
        key_sum,
        value_sum,
        b_value_sum,
        out_sum,
        vector_sums[0],
        vector_sums[1],
        vector_sums[2],
        up_sum,
        b_up_sum,
        down_sum,
        vector_sums[3],
        vector_sums[4],
        vector_sums[5],
    )


def solution(mesh):
    return jax.shard_map(
        on_device,
        mesh=mesh,
        in_specs=(
            P(None, "dp", "tensor"),
            P(),
            P(),
            P(None, "tensor"),
            P("tensor"),
            P(None, "tensor"),
            P(None, "tensor"),
            P("tensor"),
            P("tensor", None),
            P("tensor"),
            P("tensor"),
            P("tensor"),
            P(None, "tensor"),
            P("tensor"),
            P("tensor", None),
            P("tensor"),
            P("tensor"),
            P("tensor"),
            P("dp", "tensor", None),
        ),
        out_specs=(
            P("dp", "tensor", None),
            P(None, "dp", "tensor"),
            P(None, "tensor"),
            P("tensor"),
            P(None, "tensor"),
            P(None, "tensor"),
            P("tensor"),
            P("tensor", None),
            P("tensor"),
            P("tensor"),
            P("tensor"),
            P(None, "tensor"),
            P("tensor"),
            P("tensor", None),
            P("tensor"),
            P("tensor"),
            P("tensor"),
        ),
        check_vma=False,
    )
```

time: 798 us -> 477 us (0.60)
  waiting for transfers between devices: 364 us -> 57.5 us
  blocking collectives: 130 us -> 29.5 us
  starting transfers between devices: 7.87 us -> 64.6 us
  local copies, waits for them, and re-layouts: 39.5 us -> 78.9 us
  between operations: 15.4 us -> 2.54 us
  other arithmetic: 46.5 us -> 56.3 us
  matrix products: 186 us -> 178 us
    psum x1 -> x0, waiting for transfers between devices: 290 us -> none  [on_device(): lax.psum((grad_w_query, grad_b_query, grad_w_key, grad_w_value, grad_b_va...]
    psum x1 -> x0, blocking collectives: 98 us -> none  [on_device(): lax.psum((grad_w_query, grad_b_query, grad_w_key, grad_w_value, grad_b_va...]
    ppermute x0 -> x62, starting transfers between devices: none -> 59.6 us  [the longest x52 56.9 us: across(): return lax.ppermute(value, 'dp', [(i, i ^ 1 << bit) for i in range(count)])]
    ppermute x0 -> x62, waiting for transfers between devices: none -> 57.5 us  [the longest x52 55.4 us: across(): return lax.ppermute(value, 'dp', [(i, i ^ 1 << bit) for i in range(count)])]
    all_gather x4 -> x0, waiting for transfers between devices: 38.8 us -> none  [the longest x1 11.2 us: on_device(): normed_all = lax.all_gather(normed_low, 'tensor', axis=1, tiled=True)]
    reduce_scatter x3 -> x0, waiting for transfers between devices: 35 us -> none  [the longest x1 12.4 us: on_device(): lax.psum_scatter(normed_terms, 'tensor', scatter_dimension=1, tiled=True)]
    dynamic_update_slice x0 -> x42, local copies, waits for them, and re-layouts: none -> 31.8 us  [the longest x18 16.1 us: gather_back(): joined = lax.dynamic_update_slice_in_dim(joined, value, mine * half, 0)]
    convert_element_type x6 -> x12, other arithmetic: 1.36 us -> 16 us  [the longest x6 13.3 us: reduce_all(): return gather_back(total, bits).reshape(rows, columns).astype(f32)]
  transfers between devices with their start and end apart: 11 -> 63, of which waited for: 8 -> 24; matrix products, arithmetic and copies ran while one was open for 6% -> 50% of each run, Pallas kernels for 0% -> 0%
where the time goes in v1:
time: 477 us; the launch traced here: 468 us
  matrix products  178 us (37%)
  local copies, waits for them, and re-layouts  78.9 us (17%)
  starting transfers between devices  64.6 us (14%)
  waiting for transfers between devices  57.5 us (12%)
  other arithmetic  56.3 us (12%)
  blocking collectives  29.5 us (6%)
    dot_general x32, matrix products, product(): return jnp.einsum(form, left, right, preferred_element_type=f32)  178 us
    ppermute x52, starting transfers between devices, across(): return lax.ppermute(value, 'dp', [(i, i ^ 1 << bit) for i in range(count)])  56.9 us
    ppermute x52, waiting for transfers between devices, across(): return lax.ppermute(value, 'dp', [(i, i ^ 1 << bit) for i in range(count)])  55.4 us
    all_to_all x1, blocking collectives, on_device(): lax.all_to_all(inputs[order], 'dp', split_axis=0, concat_axis=1, tiled=True)  29.5 us
    dynamic_update_slice x18, local copies, waits for them, and re-layouts, gather_back(): joined = lax.dynamic_update_slice_in_dim(joined, value, mine * half, 0)  16.1 us
    dynamic_update_slice x24, local copies, waits for them, and re-layouts, gather_back(): value = lax.dynamic_update_slice_in_dim(joined, got, (1 - mine) * half, 0)  15.7 us
    unnamed x140, local copies, waits for them, and re-layouts  15.1 us
    convert_element_type x6, other arithmetic, reduce_all(): return gather_back(total, bits).reshape(rows, columns).astype(f32)  13.3 us
  transfers between devices with their start and end apart: 63, of which 24 were waited for; matrix products, arithmetic and copies ran while one was open for 50% of the time, Pallas kernels for 0%

profile of v1, /device:TPU:0, one launch (start us, length us, event | category | flops | bytes accessed | tf_op | source)
XLA Modules:
  0.0 467.5 jit_solution(7331140188777842473)
XLA Ops:
  3.4 29.5 %all_to_all.21 = bf16[16,64,384]{2,1,0:T(8,128)(2,1)} all-to-all(bf16[16,64,384]{2,1,0:T(8,128)(2,1)S(1)} %gather_fusion), channel_id=1, replica_groups=mesh['dp'=16,'tensor'=2] {'dp'}, dimensions={0} | all-to-all | bytes 1572864 | tf_op jit(solution)/shard_map/all_to_all | solution.py:154
  39.2 10.7 %fusion.3 = (f32[6,1024]{1,0:T(8,128)S(1)}, f32[6,1024,1024]{1,2,0:T(8,128)}) fusion(pred[1024]{0:T(1024)(128)(4,1)S(1)} %fusion.104, bf16[1024,6,64]{0,2,1:T(8,128)(2,1)S(1)} %bitcast.182, bf16[1024,6,64]{0,2,1:T(8,128)(2,1)S(1)} %bitcast.180), kind=kOutput, calls=%fused_computation.13 | convolution fusion | flops 824174592 | bytes 26764288 | tf_op jit(solution)/shard_map/qhd,khd->hqk/dot_general | solution.py:24
  49.9 11.8 %fusion.2 = f32[6,1024]{1,0:T(8,128)S(1)} fusion(f32[6,1024,1024]{1,2,0:T(8,128)} %get-tuple-element.77, f32[6,1024]{1,0:T(8,128)S(1)} %get-tuple-element.76, pred[1024]{0:T(1024)(128)(4,1)S(1)} %fusion.104), kind=kLoop, calls=%fused_computation.12 | loop fusion | flops 25159680 | bytes 25216000 | tf_op jit(solution)/shard_map/reduce_sum | solution.py:36
  62.6 12.0 %fusion.76 = bf16[6,64,1024]{2,1,0:T(8,128)(2,1)S(1)} fusion(bf16[1024,6,64]{0,2,1:T(8,128)(2,1)S(1)} %bitcast.176, f32[6,1024,1024]{1,2,0:T(8,128)} %get-tuple-element.77, f32[6,1024]{1,0:T(8,128)S(1)} %fusion.2, f32[6,1024]{1,0:T(8,128)S(1)} %get-tuple-element.76, pred[1024]{0:T(1024)(128)(4,1)S(1)} %fusion.104), kind=kOutput, calls=%fused_computation.122 | convolution fusion | flops 837156864 | bytes 26788864 | tf_op jit(solution)/shard_map/hqk,khd->qhd/dot_general | solution.py:24
  82.3 2.4 fusion.139
  89.7 8.8 %multiply_convert_fusion.1 = (bf16[512,1536]{1,0:T(8,128)(2,1)S(1)}, f32[512,1536]{1,0:T(8,128)S(1)}, f32[512,1536]{1,0:T(8,128)S(1)}) fusion(f32[1536]{0:T(1024)S(1)} %convert_element_type.340, bf16[512,768]{1,0:T(8,128)(2,1)} %collective-permute-done.3, bf16[768,1536]{1,0:T(8,128)(2,1)S(1)} %copy-done), kind=kOutput, calls=%fused_computation.44 | convolution fusion | flops 1259864064 | bytes 11016192 | tf_op jit(solution)/shard_map/nd,df->nf/dot_general | solution.py:24
  100.3 9.2 %multiply_convert_fusion.2 = (bf16[512,1536]{1,0:T(8,128)(2,1)S(1)}, f32[512,1536]{1,0:T(8,128)S(1)}, f32[512,1536]{1,0:T(8,128)S(1)}) fusion(f32[1536]{0:T(1024)S(1)} %convert_element_type.340, bf16[512,768]{1,0:T(8,128)(2,1)} %fusion.77, bf16[768,1536]{1,0:T(8,128)(2,1)S(1)} %copy-done), kind=kOutput, calls=%fused_computation.57 | convolution fusion | flops 1259864064 | bytes 11016192 | tf_op jit(solution)/shard_map/nd,df->nf/dot_general | solution.py:24
  114.6 2.3 fusion.133
  116.9 2.3 fusion.132
  120.9 2.7 fusion.39
  126.2 4.2 fusion.35
  136.7 2.4 fusion.130
  139.1 2.6 copy.68
  143.8 9.6 %collective-permute-done.54 = bf16[8,96,768]{2,1,0:T(8,128)(2,1)} collective-permute-done((bf16[8,96,768]{2,1,0:T(8,128)(2,1)}, bf16[8,96,768]{2,1,0:T(8,128)(2,1)}, u32[]{:S(2)}, u32[]{:S(2)}) %collective-permute-start.54) | collective-permute-done | bytes 1179680 | tf_op jit(solution)/shard_map/ppermute | solution.py:61
  153.4 2.3 convert_add_fusion
  157.4 3.5 collective-permute-done.46
  160.9 2.3 convert_add_fusion.1
  167.6 10.2 %fusion.143 = f32[6,1024,1024]{1,2,0:T(8,128)} fusion(bf16[1024,6,64]{0,2,1:T(8,128)(2,1)S(1)} %bitcast.178, bf16[1024,6,64]{0,2,1:T(8,128)(2,1)S(1)} %bitcast.177), kind=kOutput, calls=%fused_computation.325 | convolution fusion | flops 805306368 | bytes 26738688 | tf_op jit(solution)/shard_map/qhd,khd->hqk/dot_general | solution.py:24
  177.8 11.4 %convert_reduce_fusion.1 = (f32[6,64]{1,0:T(8,128)S(1)}, bf16[6,64,1024]{2,1,0:T(8,128)(2,1)S(1)}) fusion(bf16[1024,6,64]{0,2,1:T(8,128)(2,1)S(1)} %bitcast.179, f32[6,1024,1024]{1,2,0:T(8,128)} %get-tuple-element.77, f32[6,1024]{1,0:T(8,128)S(1)} %log_add_fusion, pred[1024]{0:T(1024)(128)(4,1)S(1)} %copy-done.55), kind=kOutput, calls=%fused_computation.99 | convolution fusion | flops 831651456 | bytes 26765824 | tf_op jit(solution)/shard_map/hqk,qhd->khd/dot_general | solution.py:24
  189.2 35.1 %fusion.73 = bf16[6,64,1024]{2,1,0:T(8,128)(2,1)} fusion(bf16[1024,6,64]{0,2,1:T(8,128)(2,1)} %bitcast.183, f32[6,1024,1024]{1,2,0:T(8,128)} %fusion.143, f32[6,1024,1024]{1,2,0:T(8,128)} %get-tuple-element.77, f32[6,1024]{1,0:T(8,128)S(1)} %log_add_fusion, pred[1024]{0:T(1024)(128)(4,1)S(1)} %copy-done.55), kind=kOutput, calls=%fused_computation.118 | convolution fusion | flops 874912768 | bytes 51930112 | tf_op jit(solution)/shard_map/hqk,qhd->khd/dot_general | solution.py:24
  224.3 35.1 %convert_reduce_fusion.2 = (f32[6,64]{1,0:T(8,128)S(1)}, bf16[6,64,1024]{2,1,0:T(8,128)(2,1)}) fusion(bf16[1024,6,64]{0,2,1:T(8,128)(2,1)} %bitcast.181, f32[6,1024,1024]{1,2,0:T(8,128)} %fusion.143, f32[6,1024,1024]{1,2,0:T(8,128)} %get-tuple-element.77, f32[6,1024]{1,0:T(8,128)S(1)} %log_add_fusion, pred[1024]{0:T(1024)(128)(4,1)S(1)} %copy-done.55), kind=kOutput, calls=%fused_computation.100 | convolution fusion | flops 875698816 | bytes 51931648 | tf_op jit(solution)/shard_map/hqk,khd->qhd/dot_general | solution.py:24
  259.5 3.2 fusion.86
  262.7 2.9 fusion.91
  278.4 2.9 fusion.144
  286.3 2.4 collective-permute-done.19
  289.7 2.8 collective-permute-done.20
  293.1 4.1 collective-permute-done.21
  309.9 3.6 collective-permute-done.39
  315.4 3.2 collective-permute-done.23
  330.0 9.4 %collective-permute-done.41 = bf16[1,24,768]{2,1,0:T(8,128)(2,1)S(1)} collective-permute-done((bf16[1,24,768]{2,1,0:T(8,128)(2,1)S(1)}, bf16[1,24,768]{2,1,0:T(8,128)(2,1)S(1)}, u32[]{:S(2)}, u32[]{:S(2)}) %collective-permute-start.41) | collective-permute-done | bytes 36896 | tf_op jit(solution)/shard_map/ppermute | solution.py:61
  340.2 2.2 collective-permute-start.12
  345.3 2.4 collective-permute-start.34
  350.7 2.9 collective-permute-start.13
  356.3 2.1 collective-permute-start.35
  364.1 2.5 collective-permute-start.50
  379.9 2.4 copy.84
  382.8 6.4 %reduce.15 = bf16[1024,384]{1,0:T(8,128)(2,1)S(1)} reduce(bf16[1024,1,384]{2,1,0:T(2,128)(2,1)} %bitcast.155, bf16[]{:T(256)} %broadcast.501), dimensions={1}, to_apply=%bitcast.154.reduce_sub_computation | reduce | bytes 1572866
  390.3 5.0 %all-to-all-start.1 = ((bf16[16,2,12288]{2,1,0:T(2,128)(2,1)}), bf16[16,2,12288]{2,1,0:T(2,128)(2,1)}, u32[]{:S(2)}, u32[]{:S(2)}) async-start(bf16[16,2,12288]{2,1,0:T(2,128)(2,1)} %reshape.350), calls=%async_computation.1 | async-start | bytes 1572864 | tf_op jit(solution)/shard_map/all_to_all | solution.py:244
  422.0 6.5 %collective-permute-done.60 = bf16[4,96,768]{2,1,0:T(8,128)(2,1)S(1)} collective-permute-done((bf16[4,96,768]{2,1,0:T(8,128)(2,1)S(1)}, bf16[4,96,768]{2,1,0:T(8,128)(2,1)S(1)}, u32[]{:S(2)}, u32[]{:S(2)}) %collective-permute-start.60) | collective-permute-done | bytes 589856 | tf_op jit(solution)/shard_map/ppermute | solution.py:61
  438.5 2.4 constant_dynamic-update-slice_fusion.9
  440.9 5.2 %reshape.351 = bf16[1024,1,384]{2,1,0:T(2,128)(2,1)} reshape(bf16[16,2,12288]{2,1,0:T(2,128)(2,1)} %all-to-all-done.1) | data formatting | bytes 1572864
  446.2 2.4 copy.82
  448.6 2.8 gather_fusion.2
  451.3 2.5 collective-permute-done.61
  453.9 2.4 constant_dynamic-update-slice_fusion
  456.2 4.2 bitcast_convert_fusion
  460.4 2.4 constant_dynamic-update-slice_fusion.8
  462.8 4.5 bitcast_convert_fusion.1
  (446 shorter events, 158.7 us)
Async XLA Ops:
  99.9 9.7 %collective-permute-start.4 = (bf16[512,768]{1,0:T(8,128)(2,1)S(1)}, bf16[512,768]{1,0:T(8,128)(2,1)S(1)}, u32[]{:S(2)}, u32[]{:S(2)}) collective-permute-start(bf16[512,768]{1,0:T(8,128)(2,1)S(1)} %convolution_convert_fusion.3), channel_id=1, source_target_pairs={{0,1},{1,0},{2,3},{3,2},{4,5},{5,4},{6,7},{7,6},{8,9},{9,8},{10,11... | collective-permute-start | bytes 2359304 | tf_op jit(solution)/shard_map/ppermute | solution.py:56
  120.6 11.9 %collective-permute-start.6 = (bf16[512,768]{1,0:T(8,128)(2,1)S(1)}, bf16[512,768]{1,0:T(8,128)(2,1)S(1)}, u32[]{:S(2)}, u32[]{:S(2)}) collective-permute-start(bf16[512,768]{1,0:T(8,128)(2,1)S(1)} %convolution_convert_fusion.2), channel_id=1, source_target_pairs={{0,1},{1,0},{2,3},{3,2},{4,5},{5,4},{6,7},{7,6},{8,9},{9,8},{10,11... | collective-permute-start | bytes 2359304 | tf_op jit(solution)/shard_map/ppermute | solution.py:56
  125.0 28.4 %collective-permute-start.54 = (bf16[8,96,768]{2,1,0:T(8,128)(2,1)}, bf16[8,96,768]{2,1,0:T(8,128)(2,1)}, u32[]{:S(2)}, u32[]{:S(2)}) collective-permute-start(bf16[8,96,768]{2,1,0:T(8,128)(2,1)} %dynamic-slice_convert_fusion), channel_id=1, source_target_pairs={{0,2},{2,0},{4,6},{6,4},{8,10},{10,8},{12,14},{14,12},{16,18},{18,... | collective-permute-start | bytes 3538952 | tf_op jit(solution)/shard_map/ppermute | solution.py:61
  131.8 29.2 %collective-permute-start.46 = (bf16[8,48,1536]{2,1,0:T(8,128)(2,1)}, bf16[8,48,1536]{2,1,0:T(8,128)(2,1)}, u32[]{:S(2)}, u32[]{:S(2)}) collective-permute-start(bf16[8,48,1536]{2,1,0:T(8,128)(2,1)} %dynamic-slice_convert_fusion.1), channel_id=1, source_target_pairs={{0,4},{2,6},{4,0},{6,2},{8,12},{10,14},{12,8},{14,10},{16,20},{18,... | collective-permute-start | bytes 3538952 | tf_op jit(solution)/shard_map/ppermute | solution.py:61
  136.6 7.2 %collective-permute-start.17 = (f32[6,384]{1,0:T(8,128)S(1)}, f32[6,384]{1,0:T(8,128)S(1)}, u32[]{:S(2)}, u32[]{:S(2)}) collective-permute-start(f32[6,384]{1,0:T(8,128)S(1)} %constant_dynamic-slice_fusion), channel_id=1, source_target_pairs={{0,1},{1,0},{2,3},{3,2},{4,5},{5,4},{6,7},{7,6},{8,9},{9,8},{10,11... | collective-permute-start | bytes 27656 | tf_op jit(solution)/shard_map/ppermute | solution.py:56
  143.2 22.4 %collective-permute-start.7 = (bf16[512,768]{1,0:T(8,128)(2,1)S(1)}, bf16[512,768]{1,0:T(8,128)(2,1)}, u32[]{:S(2)}, u32[]{:S(2)}) collective-permute-start(bf16[512,768]{1,0:T(8,128)(2,1)S(1)} %convert_element_type.353), channel_id=1, source_target_pairs={{0,1},{1,0},{2,3},{3,2},{4,5},{5,4},{6,7},{7,6},{8,9},{9,8},{10,11... | collective-permute-start | bytes 2359304 | tf_op jit(solution)/shard_map/ppermute | solution.py:56
  156.7 143.1 %collective-permute-start.55 = (bf16[4,96,768]{2,1,0:T(8,128)(2,1)}, bf16[4,96,768]{2,1,0:T(8,128)(2,1)}, u32[]{:S(2)}, u32[]{:S(2)}) collective-permute-start(bf16[4,96,768]{2,1,0:T(8,128)(2,1)} %dynamic-slice_convert_fusion.2), channel_id=1, source_target_pairs={{0,4},{2,6},{4,0},{6,2},{8,12},{10,14},{12,8},{14,10},{16,20},{18,... | collective-permute-start | bytes 1769480 | tf_op jit(solution)/shard_map/ppermute | solution.py:61
  164.9 137.1 %collective-permute-start.47 = (bf16[4,48,1536]{2,1,0:T(8,128)(2,1)}, bf16[4,48,1536]{2,1,0:T(8,128)(2,1)}, u32[]{:S(2)}, u32[]{:S(2)}) collective-permute-start(bf16[4,48,1536]{2,1,0:T(8,128)(2,1)} %dynamic-slice_convert_fusion.3), channel_id=1, source_target_pairs={{0,2},{2,0},{4,6},{6,4},{8,10},{10,8},{12,14},{14,12},{16,18},{18,... | collective-permute-start | bytes 1769480 | tf_op jit(solution)/shard_map/ppermute | solution.py:61
  272.3 31.2 %collective-permute-start.38 = (bf16[8,24,768]{2,1,0:T(8,128)(2,1)}, bf16[8,24,768]{2,1,0:T(8,128)(2,1)}, u32[]{:S(2)}, u32[]{:S(2)}) collective-permute-start(bf16[8,24,768]{2,1,0:T(8,128)(2,1)} %dynamic-slice_convert_fusion.6), channel_id=1, source_target_pairs={{0,2},{2,0},{4,6},{6,4},{8,10},{10,8},{12,14},{14,12},{16,18},{18,... | collective-permute-start | bytes 884744 | tf_op jit(solution)/shard_map/ppermute | solution.py:61
  274.6 30.9 %collective-permute-start.30 = (bf16[8,48,384]{2,1,0:T(8,128)(2,1)S(1)}, bf16[8,48,384]{2,1,0:T(8,128)(2,1)}, u32[]{:S(2)}, u32[]{:S(2)}) collective-permute-start(bf16[8,48,384]{2,1,0:T(8,128)(2,1)S(1)} %dynamic-slice_convert_fusion.7), channel_id=1, source_target_pairs={{0,4},{2,6},{4,0},{6,2},{8,12},{10,14},{12,8},{14,10},{16,20},{18,... | collective-permute-start | bytes 884744 | tf_op jit(solution)/shard_map/ppermute | solution.py:61
  277.6 7.2 %collective-permute-start.18 = (f32[36,128]{1,0:T(8,128)S(1)}, f32[36,128]{1,0:T(8,128)S(1)}, u32[]{:S(2)}, u32[]{:S(2)}) collective-permute-start(f32[36,128]{1,0:T(8,128)S(1)} %maximum_bitcast_fusion), channel_id=1, source_target_pairs={{0,2},{2,0},{4,6},{6,4},{8,10},{10,8},{12,14},{14,12},{16,18},{18,... | collective-permute-start | bytes 55304 | tf_op jit(solution)/shard_map/ppermute | solution.py:61
  297.2 10.5 %collective-permute-start.22 = (bf16[8,48,384]{2,1,0:T(8,128)(2,1)S(1)}, bf16[8,48,384]{2,1,0:T(8,128)(2,1)S(1)}, u32[]{:S(2)}, u32[]{:S(2)}) collective-permute-start(bf16[8,48,384]{2,1,0:T(8,128)(2,1)S(1)} %dynamic-slice_convert_fusion.8), channel_id=1, source_target_pairs={{0,4},{2,6},{4,0},{6,2},{8,12},{10,14},{12,8},{14,10},{16,20},{18,... | collective-permute-start | bytes 884744 | tf_op jit(solution)/shard_map/ppermute | solution.py:61
  299.7 8.9 %collective-permute-start.9 = (bf16[8,48,384]{2,1,0:T(8,128)(2,1)S(1)}, bf16[8,48,384]{2,1,0:T(8,128)(2,1)S(1)}, u32[]{:S(2)}, u32[]{:S(2)}) collective-permute-start(bf16[8,48,384]{2,1,0:T(8,128)(2,1)S(1)} %dynamic-slice_convert_fusion.9), channel_id=1, source_target_pairs={{0,2},{2,0},{4,6},{6,4},{8,10},{10,8},{12,14},{14,12},{16,18},{18,... | collective-permute-start | bytes 884744 | tf_op jit(solution)/shard_map/ppermute | solution.py:61
  302.0 76.8 %collective-permute-start.8 = (bf16[1024,384]{1,0:T(8,128)(2,1)S(1)}, bf16[1024,384]{1,0:T(8,128)(2,1)S(1)}, u32[]{:S(2)}, u32[]{:S(2)}) collective-permute-start(bf16[1024,384]{1,0:T(8,128)(2,1)S(1)} %pad_maximum_fusion.4), channel_id=1, source_target_pairs={{0,1},{1,0},{2,3},{3,2},{4,5},{5,4},{6,7},{7,6},{8,9},{9,8},{10,11... | collective-permute-start | bytes 2359304 | tf_op jit(solution)/shard_map/ppermute | solution.py:56
  303.5 18.5 %collective-permute-start.56 = (bf16[2,96,768]{2,1,0:T(8,128)(2,1)S(1)}, bf16[2,96,768]{2,1,0:T(8,128)(2,1)S(1)}, u32[]{:S(2)}, u32[]{:S(2)}) collective-permute-start(bf16[2,96,768]{2,1,0:T(8,128)(2,1)S(1)} %dynamic-slice_convert_fusion.4), channel_id=1, source_target_pairs={{0,8},{2,10},{4,12},{6,14},{8,0},{10,2},{12,4},{14,6},{16,24},{18,... | collective-permute-start | bytes 884744 | tf_op jit(solution)/shard_map/ppermute | solution.py:61
  305.5 15.3 %collective-permute-start.48 = (bf16[2,48,1536]{2,1,0:T(8,128)(2,1)S(1)}, bf16[2,48,1536]{2,1,0:T(8,128)(2,1)S(1)}, u32[]{:S(2)}, u32[]{:S(2)}) collective-permute-start(bf16[2,48,1536]{2,1,0:T(8,128)(2,1)S(1)} %dynamic-slice_convert_fusion.5), channel_id=1, source_target_pairs={{0,8},{2,10},{4,12},{6,14},{8,0},{10,2},{12,4},{14,6},{16,24},{18,... | collective-permute-start | bytes 884744 | tf_op jit(solution)/shard_map/ppermute | solution.py:61
  307.8 5.7 %collective-permute-start.39 = (bf16[4,24,768]{2,1,0:T(8,128)(2,1)S(1)}, bf16[4,24,768]{2,1,0:T(8,128)(2,1)S(1)}, u32[]{:S(2)}, u32[]{:S(2)}) collective-permute-start(bf16[4,24,768]{2,1,0:T(8,128)(2,1)S(1)} %dynamic-slice_convert_fusion.12), channel_id=1, source_target_pairs={{0,4},{2,6},{4,0},{6,2},{8,12},{10,14},{12,8},{14,10},{16,20},{18,... | collective-permute-start | bytes 442376 | tf_op jit(solution)/shard_map/ppermute | solution.py:61
  308.7 5.9 %collective-permute-start.31 = (bf16[4,48,384]{2,1,0:T(8,128)(2,1)S(1)}, bf16[4,48,384]{2,1,0:T(8,128)(2,1)S(1)}, u32[]{:S(2)}, u32[]{:S(2)}) collective-permute-start(bf16[4,48,384]{2,1,0:T(8,128)(2,1)S(1)} %dynamic-slice_convert_fusion.13), channel_id=1, source_target_pairs={{0,2},{2,0},{4,6},{6,4},{8,10},{10,8},{12,14},{14,12},{16,18},{18,... | collective-permute-start | bytes 442376 | tf_op jit(solution)/shard_map/ppermute | solution.py:61
  319.7 5.6 %collective-permute-start.32 = (bf16[2,48,384]{2,1,0:T(8,128)(2,1)S(1)}, bf16[2,48,384]{2,1,0:T(8,128)(2,1)S(1)}, u32[]{:S(2)}, u32[]{:S(2)}) collective-permute-start(bf16[2,48,384]{2,1,0:T(8,128)(2,1)S(1)} %dynamic-slice_convert_fusion.17), channel_id=1, source_target_pairs={{0,8},{2,10},{4,12},{6,14},{8,0},{10,2},{12,4},{14,6},{16,24},{18,... | collective-permute-start | bytes 221192 | tf_op jit(solution)/shard_map/ppermute | solution.py:61
  320.9 6.1 %collective-permute-start.24 = (bf16[2,48,384]{2,1,0:T(8,128)(2,1)S(1)}, bf16[2,48,384]{2,1,0:T(8,128)(2,1)S(1)}, u32[]{:S(2)}, u32[]{:S(2)}) collective-permute-start(bf16[2,48,384]{2,1,0:T(8,128)(2,1)S(1)} %dynamic-slice_convert_fusion.18), channel_id=1, source_target_pairs={{0,8},{2,10},{4,12},{6,14},{8,0},{10,2},{12,4},{14,6},{16,24},{18,... | collective-permute-start | bytes 221192 | tf_op jit(solution)/shard_map/ppermute | solution.py:61
  322.0 6.5 %collective-permute-start.11 = (bf16[2,48,384]{2,1,0:T(8,128)(2,1)S(1)}, bf16[2,48,384]{2,1,0:T(8,128)(2,1)S(1)}, u32[]{:S(2)}, u32[]{:S(2)}) collective-permute-start(bf16[2,48,384]{2,1,0:T(8,128)(2,1)S(1)} %dynamic-slice_convert_fusion.19), channel_id=1, source_target_pairs={{0,8},{2,10},{4,12},{6,14},{8,0},{10,2},{12,4},{14,6},{16,24},{18,... | collective-permute-start | bytes 221192 | tf_op jit(solution)/shard_map/ppermute | solution.py:61
  323.7 36.0 %collective-permute-start.57 = (bf16[1,96,768]{2,1,0:T(8,128)(2,1)S(1)}, bf16[1,96,768]{2,1,0:T(8,128)(2,1)S(1)}, u32[]{:S(2)}, u32[]{:S(2)}) collective-permute-start(bf16[1,96,768]{2,1,0:T(8,128)(2,1)S(1)} %dynamic-slice_convert_fusion.10), channel_id=1, source_target_pairs={{0,16},{2,18},{4,20},{6,22},{8,24},{10,26},{12,28},{14,30},{16,0},... | collective-permute-start | bytes 442376 | tf_op jit(solution)/shard_map/ppermute | solution.py:61
  325.3 34.3 %collective-permute-start.49 = (bf16[1,48,1536]{2,1,0:T(8,128)(2,1)S(1)}, bf16[1,48,1536]{2,1,0:T(8,128)(2,1)S(1)}, u32[]{:S(2)}, u32[]{:S(2)}) collective-permute-start(bf16[1,48,1536]{2,1,0:T(8,128)(2,1)S(1)} %dynamic-slice_convert_fusion.11), channel_id=1, source_target_pairs={{0,16},{2,18},{4,20},{6,22},{8,24},{10,26},{12,28},{14,30},{16,0},... | collective-permute-start | bytes 442376 | tf_op jit(solution)/shard_map/ppermute | solution.py:61
  326.9 12.5 %collective-permute-start.41 = (bf16[1,24,768]{2,1,0:T(8,128)(2,1)S(1)}, bf16[1,24,768]{2,1,0:T(8,128)(2,1)S(1)}, u32[]{:S(2)}, u32[]{:S(2)}) collective-permute-start(bf16[1,24,768]{2,1,0:T(8,128)(2,1)S(1)} %dynamic-slice_convert_fusion.20), channel_id=1, source_target_pairs={{0,16},{2,18},{4,20},{6,22},{8,24},{10,26},{12,28},{14,30},{16,0},... | collective-permute-start | bytes 110600 | tf_op jit(solution)/shard_map/ppermute | solution.py:61
  328.5 11.7 %collective-permute-start.33 = (bf16[1,48,384]{2,1,0:T(8,128)(2,1)S(1)}, bf16[1,48,384]{2,1,0:T(8,128)(2,1)S(1)}, u32[]{:S(2)}, u32[]{:S(2)}) collective-permute-start(bf16[1,48,384]{2,1,0:T(8,128)(2,1)S(1)} %dynamic-slice_convert_fusion.21), channel_id=1, source_target_pairs={{0,16},{2,18},{4,20},{6,22},{8,24},{10,26},{12,28},{14,30},{16,0},... | collective-permute-start | bytes 110600 | tf_op jit(solution)/shard_map/ppermute | solution.py:61
  349.4 5.6 %collective-permute-start.26 = (bf16[1,48,384]{2,1,0:T(8,128)(2,1)S(1)}, bf16[1,48,384]{2,1,0:T(8,128)(2,1)S(1)}, u32[]{:S(2)}, u32[]{:S(2)}) collective-permute-start(bf16[1,48,384]{2,1,0:T(8,128)(2,1)S(1)} %get-tuple-element.37), channel_id=1, source_target_pairs={{0,16},{2,18},{4,20},{6,22},{8,24},{10,26},{12,28},{14,30},{16,0},... | collective-permute-start | bytes 110600 | tf_op jit(solution)/shard_map/ppermute | solution.py:61
  350.7 5.5 %collective-permute-start.13 = (bf16[1,48,384]{2,1,0:T(8,128)(2,1)S(1)}, bf16[1,48,384]{2,1,0:T(8,128)(2,1)S(1)}, u32[]{:S(2)}, u32[]{:S(2)}) collective-permute-start(bf16[1,48,384]{2,1,0:T(8,128)(2,1)S(1)} %get-tuple-element.45), channel_id=1, source_target_pairs={{0,16},{2,18},{4,20},{6,22},{8,24},{10,26},{12,28},{14,30},{16,0},... | collective-permute-start | bytes 110600 | tf_op jit(solution)/shard_map/ppermute | solution.py:61
  354.9 7.0 %collective-permute-start.43 = (bf16[2,24,768]{2,1,0:T(8,128)(2,1)S(1)}, bf16[2,24,768]{2,1,0:T(8,128)(2,1)S(1)}, u32[]{:S(2)}, u32[]{:S(2)}) collective-permute-start(bf16[2,24,768]{2,1,0:T(8,128)(2,1)S(1)} %constant_dynamic-update-slice_fusion.22), channel_id=1, source_target_pairs={{0,8},{2,10},{4,12},{6,14},{8,0},{10,2},{12,4},{14,6},{16,24},{18,... | collective-permute-start | bytes 221192 | tf_op jit(solution)/shard_map/ppermute | solution.py:61
  356.3 7.8 %collective-permute-start.35 = (bf16[2,48,384]{2,1,0:T(8,128)(2,1)S(1)}, bf16[2,48,384]{2,1,0:T(8,128)(2,1)S(1)}, u32[]{:S(2)}, u32[]{:S(2)}) collective-permute-start(bf16[2,48,384]{2,1,0:T(8,128)(2,1)S(1)} %constant_dynamic-update-slice_fusion.30), channel_id=1, source_target_pairs={{0,8},{2,10},{4,12},{6,14},{8,0},{10,2},{12,4},{14,6},{16,24},{18,... | collective-permute-start | bytes 221192 | tf_op jit(solution)/shard_map/ppermute | solution.py:61
  359.7 8.7 %collective-permute-start.27 = (bf16[2,48,384]{2,1,0:T(8,128)(2,1)S(1)}, bf16[2,48,384]{2,1,0:T(8,128)(2,1)S(1)}, u32[]{:S(2)}, u32[]{:S(2)}) collective-permute-start(bf16[2,48,384]{2,1,0:T(8,128)(2,1)S(1)} %constant_dynamic-update-slice_fusion.38), channel_id=1, source_target_pairs={{0,8},{2,10},{4,12},{6,14},{8,0},{10,2},{12,4},{14,6},{16,24},{18,... | collective-permute-start | bytes 221192 | tf_op jit(solution)/shard_map/ppermute | solution.py:61
  359.8 12.4 %collective-permute-start.14 = (bf16[2,48,384]{2,1,0:T(8,128)(2,1)S(1)}, bf16[2,48,384]{2,1,0:T(8,128)(2,1)S(1)}, u32[]{:S(2)}, u32[]{:S(2)}) collective-permute-start(bf16[2,48,384]{2,1,0:T(8,128)(2,1)S(1)} %constant_dynamic-update-slice_fusion.46), channel_id=1, source_target_pairs={{0,8},{2,10},{4,12},{6,14},{8,0},{10,2},{12,4},{14,6},{16,24},{18,... | collective-permute-start | bytes 221192 | tf_op jit(solution)/shard_map/ppermute | solution.py:61
  361.9 14.3 %collective-permute-start.58 = (bf16[1,96,768]{2,1,0:T(8,128)(2,1)S(1)}, bf16[1,96,768]{2,1,0:T(8,128)(2,1)S(1)}, u32[]{:S(2)}, u32[]{:S(2)}) collective-permute-start(bf16[1,96,768]{2,1,0:T(8,128)(2,1)S(1)} %get-tuple-element.29), channel_id=1, source_target_pairs={{0,16},{2,18},{4,20},{6,22},{8,24},{10,26},{12,28},{14,30},{16,0},... | collective-permute-start | bytes 442376 | tf_op jit(solution)/shard_map/ppermute | solution.py:61
  364.1 13.2 %collective-permute-start.50 = (bf16[1,48,1536]{2,1,0:T(8,128)(2,1)S(1)}, bf16[1,48,1536]{2,1,0:T(8,128)(2,1)S(1)}, u32[]{:S(2)}, u32[]{:S(2)}) collective-permute-start(bf16[1,48,1536]{2,1,0:T(8,128)(2,1)S(1)} %get-tuple-element.31), channel_id=1, source_target_pairs={{0,16},{2,18},{4,20},{6,22},{8,24},{10,26},{12,28},{14,30},{16,0},... | collective-permute-start | bytes 442376 | tf_op jit(solution)/shard_map/ppermute | solution.py:61
  368.4 26.9 %collective-permute-start.44 = (bf16[4,24,768]{2,1,0:T(8,128)(2,1)}, bf16[4,24,768]{2,1,0:T(8,128)(2,1)}, u32[]{:S(2)}, u32[]{:S(2)}) collective-permute-start(bf16[4,24,768]{2,1,0:T(8,128)(2,1)} %constant_dynamic-update-slice_fusion.20), channel_id=1, source_target_pairs={{0,4},{2,6},{4,0},{6,2},{8,12},{10,14},{12,8},{14,10},{16,20},{18,... | collective-permute-start | bytes 442376 | tf_op jit(solution)/shard_map/ppermute | solution.py:61
  372.2 27.9 %collective-permute-start.36 = (bf16[4,48,384]{2,1,0:T(8,128)(2,1)}, bf16[4,48,384]{2,1,0:T(8,128)(2,1)}, u32[]{:S(2)}, u32[]{:S(2)}) collective-permute-start(bf16[4,48,384]{2,1,0:T(8,128)(2,1)} %constant_dynamic-update-slice_fusion.28), channel_id=1, source_target_pairs={{0,2},{2,0},{4,6},{6,4},{8,10},{10,8},{12,14},{14,12},{16,18},{18,... | collective-permute-start | bytes 442376 | tf_op jit(solution)/shard_map/ppermute | solution.py:61
  376.2 28.1 %collective-permute-start.28 = (bf16[4,48,384]{2,1,0:T(8,128)(2,1)}, bf16[4,48,384]{2,1,0:T(8,128)(2,1)}, u32[]{:S(2)}, u32[]{:S(2)}) collective-permute-start(bf16[4,48,384]{2,1,0:T(8,128)(2,1)} %constant_dynamic-update-slice_fusion.36), channel_id=1, source_target_pairs={{0,2},{2,0},{4,6},{6,4},{8,10},{10,8},{12,14},{14,12},{16,18},{18,... | collective-permute-start | bytes 442376 | tf_op jit(solution)/shard_map/ppermute | solution.py:61
  377.3 31.2 %collective-permute-start.15 = (bf16[4,48,384]{2,1,0:T(8,128)(2,1)}, bf16[4,48,384]{2,1,0:T(8,128)(2,1)}, u32[]{:S(2)}, u32[]{:S(2)}) collective-permute-start(bf16[4,48,384]{2,1,0:T(8,128)(2,1)} %constant_dynamic-update-slice_fusion.44), channel_id=1, source_target_pairs={{0,4},{2,6},{4,0},{6,2},{8,12},{10,14},{12,8},{14,10},{16,20},{18,... | collective-permute-start | bytes 442376 | tf_op jit(solution)/shard_map/ppermute | solution.py:61
  379.4 32.4 %collective-permute-start.59 = (bf16[2,96,768]{2,1,0:T(8,128)(2,1)S(1)}, bf16[2,96,768]{2,1,0:T(8,128)(2,1)}, u32[]{:S(2)}, u32[]{:S(2)}) collective-permute-start(bf16[2,96,768]{2,1,0:T(8,128)(2,1)S(1)} %constant_dynamic-update-slice_fusion.6), channel_id=1, source_target_pairs={{0,8},{2,10},{4,12},{6,14},{8,0},{10,2},{12,4},{14,6},{16,24},{18,... | collective-permute-start | bytes 884744 | tf_op jit(solution)/shard_map/ppermute | solution.py:61
  390.3 50.7 %all-to-all-start.1 = ((bf16[16,2,12288]{2,1,0:T(2,128)(2,1)}), bf16[16,2,12288]{2,1,0:T(2,128)(2,1)}, u32[]{:S(2)}, u32[]{:S(2)}) async-start(bf16[16,2,12288]{2,1,0:T(2,128)(2,1)} %reshape.350), calls=%async_computation.1 | async-start | bytes 1572864 | tf_op jit(solution)/shard_map/all_to_all | solution.py:244
  395.3 18.1 %collective-permute-start.51 = (bf16[2,48,1536]{2,1,0:T(8,128)(2,1)}, bf16[2,48,1536]{2,1,0:T(8,128)(2,1)S(1)}, u32[]{:S(2)}, u32[]{:S(2)}) collective-permute-start(bf16[2,48,1536]{2,1,0:T(8,128)(2,1)} %copy-done.32), channel_id=1, source_target_pairs={{0,8},{2,10},{4,12},{6,14},{8,0},{10,2},{12,4},{14,6},{16,24},{18,... | collective-permute-start | bytes 884744 | tf_op jit(solution)/shard_map/ppermute | solution.py:61
  400.1 17.0 %collective-permute-start.45 = (bf16[8,24,768]{2,1,0:T(8,128)(2,1)}, bf16[8,24,768]{2,1,0:T(8,128)(2,1)S(1)}, u32[]{:S(2)}, u32[]{:S(2)}) collective-permute-start(bf16[8,24,768]{2,1,0:T(8,128)(2,1)} %constant_dynamic-update-slice_fusion.18), channel_id=1, source_target_pairs={{0,2},{2,0},{4,6},{6,4},{8,10},{10,8},{12,14},{14,12},{16,18},{18,... | collective-permute-start | bytes 884744 | tf_op jit(solution)/shard_map/ppermute | solution.py:61
  404.3 15.5 %collective-permute-start.37 = (bf16[8,48,384]{2,1,0:T(8,128)(2,1)}, bf16[8,48,384]{2,1,0:T(8,128)(2,1)S(1)}, u32[]{:S(2)}, u32[]{:S(2)}) collective-permute-start(bf16[8,48,384]{2,1,0:T(8,128)(2,1)} %constant_dynamic-update-slice_fusion.26), channel_id=1, source_target_pairs={{0,4},{2,6},{4,0},{6,2},{8,12},{10,14},{12,8},{14,10},{16,20},{18,... | collective-permute-start | bytes 884744 | tf_op jit(solution)/shard_map/ppermute | solution.py:61
  408.5 12.7 %collective-permute-start.29 = (bf16[8,48,384]{2,1,0:T(8,128)(2,1)}, bf16[8,48,384]{2,1,0:T(8,128)(2,1)S(1)}, u32[]{:S(2)}, u32[]{:S(2)}) collective-permute-start(bf16[8,48,384]{2,1,0:T(8,128)(2,1)} %constant_dynamic-update-slice_fusion.34), channel_id=1, source_target_pairs={{0,4},{2,6},{4,0},{6,2},{8,12},{10,14},{12,8},{14,10},{16,20},{18,... | collective-permute-start | bytes 884744 | tf_op jit(solution)/shard_map/ppermute | solution.py:61
  411.8 10.2 %collective-permute-start.16 = (bf16[8,48,384]{2,1,0:T(8,128)(2,1)}, bf16[8,48,384]{2,1,0:T(8,128)(2,1)S(1)}, u32[]{:S(2)}, u32[]{:S(2)}) collective-permute-start(bf16[8,48,384]{2,1,0:T(8,128)(2,1)} %constant_dynamic-update-slice_fusion.42), channel_id=1, source_target_pairs={{0,2},{2,0},{4,6},{6,4},{8,10},{10,8},{12,14},{14,12},{16,18},{18,... | collective-permute-start | bytes 884744 | tf_op jit(solution)/shard_map/ppermute | solution.py:61
  413.4 15.1 %collective-permute-start.60 = (bf16[4,96,768]{2,1,0:T(8,128)(2,1)S(1)}, bf16[4,96,768]{2,1,0:T(8,128)(2,1)S(1)}, u32[]{:S(2)}, u32[]{:S(2)}) collective-permute-start(bf16[4,96,768]{2,1,0:T(8,128)(2,1)S(1)} %constant_dynamic-update-slice_fusion.4), channel_id=1, source_target_pairs={{0,4},{2,6},{4,0},{6,2},{8,12},{10,14},{12,8},{14,10},{16,20},{18,... | collective-permute-start | bytes 1769480 | tf_op jit(solution)/shard_map/ppermute | solution.py:61
  417.1 14.4 %collective-permute-start.52 = (bf16[4,48,1536]{2,1,0:T(8,128)(2,1)S(1)}, bf16[4,48,1536]{2,1,0:T(8,128)(2,1)S(1)}, u32[]{:S(2)}, u32[]{:S(2)}) collective-permute-start(bf16[4,48,1536]{2,1,0:T(8,128)(2,1)S(1)} %constant_dynamic-update-slice_fusion.12), channel_id=1, source_target_pairs={{0,2},{2,0},{4,6},{6,4},{8,10},{10,8},{12,14},{14,12},{16,18},{18,... | collective-permute-start | bytes 1769480 | tf_op jit(solution)/shard_map/ppermute | solution.py:61
  428.6 25.3 %collective-permute-start.61 = (bf16[8,96,768]{2,1,0:T(8,128)(2,1)S(1)}, bf16[8,96,768]{2,1,0:T(8,128)(2,1)}, u32[]{:S(2)}, u32[]{:S(2)}) collective-permute-start(bf16[8,96,768]{2,1,0:T(8,128)(2,1)S(1)} %constant_dynamic-update-slice_fusion.2), channel_id=1, source_target_pairs={{0,2},{2,0},{4,6},{6,4},{8,10},{10,8},{12,14},{14,12},{16,18},{18,... | collective-permute-start | bytes 3538952 | tf_op jit(solution)/shard_map/ppermute | solution.py:61
  432.4 28.1 %collective-permute-start.53 = (bf16[8,48,1536]{2,1,0:T(8,128)(2,1)}, bf16[8,48,1536]{2,1,0:T(8,128)(2,1)}, u32[]{:S(2)}, u32[]{:S(2)}) collective-permute-start(bf16[8,48,1536]{2,1,0:T(8,128)(2,1)} %constant_dynamic-update-slice_fusion.10), channel_id=1, source_target_pairs={{0,4},{2,6},{4,0},{6,2},{8,12},{10,14},{12,8},{14,10},{16,20},{18,... | collective-permute-start | bytes 3538952 | tf_op jit(solution)/shard_map/ppermute | solution.py:61
  (83 other events, 724.6 us)
